TPU v7x, 128 devices: a whole 4x4x4 slice. The times are simulated.
128 devices in a mesh: dp: 8 (over z, core), table: 16 (over x, y).
Axes of the slice: x: 4, y: 4, z: 4, core: 2. Of those that a mesh axis runs over, the one named last changes fastest.
Arguments:
- values: bfloat16 [16384, 1024], P('table'), may hold values from -6 to 6
- first_moment: float32 [16384, 1024], P('table'), may hold values from -2 to 2
- second_moment: float32 [16384, 1024], P('table'), may hold values from 0.01 to 1
- grads: bfloat16 [1024, 64, 1024], P(('dp', 'table')), may hold values from -6 to 6
- block_ids: int32 [128, 8], P(('dp', 'table')), may hold values from 0 to 255, as said below
- live_counts: int32 [128], P(('dp', 'table')), may hold values from 4 to 8
- step_count: int32 [1], replicated, may hold values from 1 to 19
Outputs:
- new_values: bfloat16 [16384, 1024], P('table')
- new_first: float32 [16384, 1024], P('table')
- new_second: float32 [16384, 1024], P('table')
Inputs may be any that keep to these rules, and one draw needn't show every extreme that they name: `block_ids`: device h belongs to replica h // 16. Live ids of a device are ascending and lie in blocks of different owners (owner = id // 16), so one device sends at most one live block to any owner; in every draw some owner receives a live block from every device of a replica. The live ids of one replica name at most 2 different blocks of any one owner, and exactly 2 of some owner in every replica. Ids of dead slots are arbitrary blocks.
All inputs are finite; a program needn't handle non-finite values.
Results may differ from a plain program's by a relative error of at most 0.0004.
Values may be sent and summed in bfloat16 or wider, within the bound.
A program may use at most 128 MiB of HBM per device.

v0:
```python
import jax
import jax.numpy as jnp
from jax import lax
from jax.sharding import PartitionSpec as P

BROWS = 64
SLOTS = 8
KBLK = 2


def adam_rows(values, first_moment, second_moment, row_grad, row_hits, step_count):
    touched = (row_hits > 0.0)[:, None]
    beta_one = 0.9
    beta_two = 0.99
    steps_done = step_count[0].astype(jnp.float32)
    first_next = beta_one * first_moment + (1.0 - beta_one) * row_grad
    second_next = beta_two * second_moment + (1.0 - beta_two) * row_grad * row_grad
    first_hat = first_next / (1.0 - jnp.power(jnp.float32(beta_one), steps_done))
    second_hat = second_next / (1.0 - jnp.power(jnp.float32(beta_two), steps_done))
    moved = values.astype(jnp.float32) - 0.05 * first_hat / (jnp.sqrt(second_hat) + 1e-08)
    new_values = jnp.where(touched, moved.astype(jnp.bfloat16), values)
    new_first = jnp.where(touched, first_next, first_moment)
    new_second = jnp.where(touched, second_next, second_moment)
    return (new_values, new_first, new_second)


def per_device(values, first_moment, second_moment, grads, block_ids, live_counts, step_count):
    owners = lax.axis_size("table")
    own_rows = values.shape[0]
    width = values.shape[1]
    blk_here = own_rows // BROWS
    slot_ids = block_ids[0]
    live = jnp.arange(SLOTS, dtype=jnp.int32) < live_counts[0]
    owner_of = slot_ids // blk_here
    local_block = slot_ids % blk_here
    select = (owner_of[None, :] == jnp.arange(owners, dtype=jnp.int32)[:, None]) & live[None, :]
    outgoing = jnp.einsum(
        "os,sxd->oxd", select.astype(jnp.bfloat16), grads, preferred_element_type=jnp.float32
    ).astype(jnp.bfloat16)
    select_int = select.astype(jnp.int32)
    labels = jnp.stack(
        [jnp.sum(select_int * local_block[None, :], axis=1), jnp.sum(select_int, axis=1)], axis=1
    )
    incoming, arrived = (
        lax.all_to_all(outgoing, "table", split_axis=0, concat_axis=0, tiled=True),
        lax.all_to_all(labels, "table", split_axis=0, concat_axis=0, tiled=True),
    )
    matches = (arrived[:, 0][None, :] == jnp.arange(blk_here, dtype=jnp.int32)[:, None]) & (
        arrived[:, 1][None, :] == 1
    )
    block_hits = jnp.sum(matches.astype(jnp.float32), axis=1)
    touched_block = block_hits > 0.0
    order = jnp.cumsum(touched_block.astype(jnp.int32)) - 1
    packing = (
        (order[None, :] == jnp.arange(KBLK, dtype=jnp.int32)[:, None]) & touched_block[None, :]
    ).astype(jnp.float32)
    chooser = jnp.dot(packing, matches.astype(jnp.float32), precision=lax.Precision.HIGHEST).astype(
        jnp.bfloat16
    )
    packed = jnp.einsum("ks,sxd->kxd", chooser, incoming, preferred_element_type=jnp.float32)
    block_index = jnp.arange(blk_here, dtype=jnp.float32)
    packed_ids = jnp.sum(packing * (block_index[None, :] + 1.0), axis=1) - 1.0
    packed_hits = jnp.sum(packing * block_hits[None, :], axis=1)
    all_packed, all_ids, all_hits = (
        lax.all_gather(packed, "dp", axis=0, tiled=True),
        lax.all_gather(packed_ids, "dp", axis=0, tiled=True),
        lax.all_gather(packed_hits, "dp", axis=0, tiled=True),
    )
    placing = (all_ids[None, :] == block_index[:, None]).astype(jnp.float32)
    row_grad = jnp.einsum(
        "bk,kxd->bxd", placing, all_packed, precision=lax.Precision.HIGHEST
    ).reshape(own_rows, width)
    total_hits = jnp.repeat(jnp.sum(placing * all_hits[None, :], axis=1), BROWS)
    return adam_rows(values, first_moment, second_moment, row_grad, total_hits, step_count)


def solution(mesh):
    in_specs = (
        P("table", None),
        P("table", None),
        P("table", None),
        P(("dp", "table"), None, None),
        P(("dp", "table"), None),
        P(("dp", "table")),
        P(),
    )
    out_specs = (P("table", None), P("table", None), P("table", None))
    return jax.shard_map(
        per_device, mesh=mesh, in_specs=in_specs, out_specs=out_specs, check_vma=False
    )
```

profile of v0, /device:TPU:1, one launch (start us, length us, event | category | flops | bytes accessed | tf_op | source)
XLA Modules:
  0.0 118.3 jit_solution(3008917598142463513)
XLA Ops:
  7.2 0.0 copy-start
  7.9 0.7 fusion.24
  8.6 0.1 select_reduce_fusion.1
  8.7 0.7 copy.29
  9.4 7.6 %all-to-all-start = ((s32[16,1,2]{2,1,0:T(1,128)}), s32[16,1,2]{2,1,0:T(1,128)S(1)}, u32[]{:S(2)}, u32[]{:S(2)}) async-start(s32[16,1,2]{2,1,0:T(1,128)} %copy.29), calls=%async_computation | async-start | bytes 16384 | tf_op jit(solution)/shard_map/all_to_all | solution.py:46
  17.0 0.0 copy-done
  17.0 0.9 convolution_convert_fusion
  17.9 2.5 %copy.33 = bf16[16,64,1024]{2,1,0:T(8,128)(2,1)} copy(bf16[16,64,1024]{2,0,1:T(8,128)(2,1)S(1)} %convolution_convert_fusion) | data formatting | bytes 4194304 | tf_op jit(solution)/shard_map/convert_element_type | solution.py:39
  20.4 0.0 copy-start.4
  20.4 2.9 %all-to-all-done = s32[16,1,2]{2,1,0:T(1,128)S(1)} async-done(((s32[16,1,2]{2,1,0:T(1,128)}), s32[16,1,2]{2,1,0:T(1,128)S(1)}, u32[]{:S(2)}, u32[]{:S(2)}) %all-to-all-start) | async-done | bytes 160 | tf_op jit(solution)/shard_map/all_to_all | solution.py:46
  23.3 3.9 %all-to-all-start.1 = ((bf16[16,64,1024]{2,1,0:T(8,128)(2,1)}), bf16[16,64,1024]{2,1,0:T(8,128)(2,1)S(1)}, u32[]{:S(2)}, u32[]{:S(2)}) async-start(bf16[16,64,1024]{2,1,0:T(8,128)(2,1)} %copy.33), calls=%async_computation.1 | async-start | bytes 4194304 | tf_op jit(solution)/shard_map/all_to_all | solution.py:45
  27.2 0.0 all-gather.2.cloned.1.call-start
  27.2 0.1 copy.30
  27.3 0.1 convert_reduce_fusion
  27.4 0.1 copy.31
  27.6 0.1 add_reduce_fusion
  27.7 0.1 fusion.9
  27.8 24.9 %all-to-all-done.1 = bf16[16,64,1024]{2,1,0:T(8,128)(2,1)S(1)} async-done(((bf16[16,64,1024]{2,1,0:T(8,128)(2,1)}), bf16[16,64,1024]{2,1,0:T(8,128)(2,1)S(1)}, u32[]{:S(2)}, u32[]{:S(2)}) %all-to-all-start.1) | async-done | bytes 2097184 | tf_op jit(solution)/shard_map/all_to_all | solution.py:45
  52.7 1.3 %fusion.7 = f32[2,64,1024]{2,0,1:T(2,128)S(1)} fusion(bf16[2,16,1]{1,0,2:T(2,128)(2,1)S(1)} %fusion.9, bf16[16,64,1024]{2,1,0:T(8,128)(2,1)S(1)} %all-to-all-done.1), kind=kOutput, calls=%fused_computation.10 | convolution fusion | flops 4194304 | bytes 2621504 | tf_op jit(solution)/shard_map/ks,sxd->kxd/dot_general | solution.py:60
  54.0 1.0 copy.35
  55.0 0.0 all-gather.2.cloned.1.call-update
  55.7 0.0 copy-done.4
  55.7 0.6 dynamic-slice
  57.0 0.1 select_reduce_fusion.2
  57.1 0.2 dynamic-update-slice.1
  57.4 0.1 add_dynamic-update-slice_fusion
  57.5 18.8 %all-reduce.2 = (f32[16]{0:T(128)S(1)}, f32[16]{0:T(128)S(1)}) all-reduce(f32[16]{0:T(128)S(1)} %add_dynamic-update-slice_fusion, f32[16]{0:T(128)S(1)} %dynamic-update-slice.1), channel_id=1, replica_groups=mesh['dp'=8,'table'=16] {'dp'}, use_global_device_ids=true, to_apply=%add | all-reduce | flops 32 | bytes 256
  76.2 0.1 select_reduce_fusion
  76.4 0.1 broadcast_in_dim.13
  76.4 0.1 gt.31
  76.5 15.0 %all-gather.2.cloned.1.call-done = f32[16,64,1024]{2,1,0:T(8,128)} async-done(((f32[2,64,1024]{2,1,0:T(8,128)}), f32[16,64,1024]{2,1,0:T(8,128)}) %all-gather.2.cloned.1.call-update) | async-done | bytes 4194320 | tf_op jit(solution)/shard_map/all_gather | solution.py:65
  91.5 6.6 %fusion.2 = f32[16,64,1024]{2,0,1:T(8,128)S(1)} fusion(f32[16,64,1024]{2,1,0:T(8,128)} %all-gather.2.cloned.1.call-done, f32[16]{0:T(128)S(1)} %get-tuple-element.7), kind=kOutput, calls=%fused_computation.4 | convolution fusion | flops 201326848 | bytes 8388672 | tf_op jit(solution)/shard_map/bk,kxd->bxd/dot_general | solution.py:70
  98.1 0.0 copy-start.1
  98.1 0.0 copy-start.2
  98.1 2.4 %copy.37 = f32[16,64,1024]{2,1,0:T(8,128)S(1)} copy(f32[16,64,1024]{2,0,1:T(8,128)S(1)} %fusion.2) | data formatting | bytes 8388608 | tf_op jit(solution)/shard_map/bk,kxd->bxd/dot_general | solution.py:70
  100.5 0.0 copy-done.1
  100.5 1.0 copy-done.2
  101.5 0.0 copy-start.3
  101.5 4.7 %fusion.5 = (f32[1024,1024]{1,0:T(8,128)}, f32[1024,1024]{1,0:T(8,128)}) fusion(f32[1024,1024]{1,0:T(8,128)S(1)} %copy-done.1, f32[16,64,1024]{2,1,0:T(8,128)S(1)} %copy.37, pred[1024]{0:T(1024)(128)(4,1)S(1)} %gt.31, f32[1024,1024]{1,0:T(8,128)S(1)} %copy-done.2), kind=kLoop, calls=%fused_computation.8 | loop fusion | flops 9437184 | bytes 20972544 | tf_op jit(solution)/shard_map/jit(_where)/select_n | solution.py:23
  106.3 0.0 copy-done.3
  106.3 5.2 %fusion.6 = bf16[1024,1024]{1,0:T(8,128)(2,1)} fusion(bf16[1024,1024]{1,0:T(8,128)(2,1)S(1)} %copy-done.3, f32[1024,1024]{1,0:T(8,128)S(1)} %copy-done.1, f32[16,64,1024]{2,1,0:T(8,128)S(1)} %copy.37, f32[1024,1024]{1,0:T(8,128)S(1)} %copy-done.2, f32[]{:T(128)} %bitcast.16, f32[]{:T(128)} %bitcast.15, pred[1024]{0:T(1024)(128)(4,1)S(1)} %gt.31), kind=kLoop, calls=%fused_computation.9 | loop fusion | flops 16777216 | bytes 16778248 | tf_op jit(solution)/shard_map/jit(_where)/select_n | solution.py:21
  (10 shorter events, 0.1 us)
Async XLA Ops:
  7.2 9.8 %copy-start = (bf16[8,64,1024]{2,1,0:T(8,128)(2,1)S(1)}, bf16[8,64,1024]{2,1,0:T(8,128)(2,1)}, u32[]{:S(2)}) copy-start(bf16[8,64,1024]{2,1,0:T(8,128)(2,1)} %param.10) | copy-start | bytes 3145732
  9.4 13.9 %all-to-all-start = ((s32[16,1,2]{2,1,0:T(1,128)}), s32[16,1,2]{2,1,0:T(1,128)S(1)}, u32[]{:S(2)}, u32[]{:S(2)}) async-start(s32[16,1,2]{2,1,0:T(1,128)} %copy.29), calls=%async_computation | async-start | bytes 16384 | tf_op jit(solution)/shard_map/all_to_all | solution.py:46
  20.4 35.3 %copy-start.4 = (u32[128]{0:T(128)S(1)}, u32[128]{0:T(128)}, u32[]{:S(2)}) copy-start(u32[128]{0:T(128)} %constant.75) | copy-start | bytes 1540
  23.3 29.4 %all-to-all-start.1 = ((bf16[16,64,1024]{2,1,0:T(8,128)(2,1)}), bf16[16,64,1024]{2,1,0:T(8,128)(2,1)S(1)}, u32[]{:S(2)}, u32[]{:S(2)}) async-start(bf16[16,64,1024]{2,1,0:T(8,128)(2,1)} %copy.33), calls=%async_computation.1 | async-start | bytes 4194304 | tf_op jit(solution)/shard_map/all_to_all | solution.py:45
  27.2 64.3 %all-gather.2.cloned.1.call-start = ((), (), s32[]{:S(2)}) async-start(), calls=%async_computation.2 | async-start | bytes 4718592 | tf_op jit(solution)/shard_map/all_gather | solution.py:65
  98.1 2.5 %copy-start.1 = (f32[1024,1024]{1,0:T(8,128)S(1)}, f32[1024,1024]{1,0:T(8,128)}, u32[]{:S(2)}) copy-start(f32[1024,1024]{1,0:T(8,128)} %param.9) | copy-start | bytes 12582916
  98.1 3.5 %copy-start.2 = (f32[1024,1024]{1,0:T(8,128)S(1)}, f32[1024,1024]{1,0:T(8,128)}, u32[]{:S(2)}) copy-start(f32[1024,1024]{1,0:T(8,128)} %param.8) | copy-start | bytes 12582916
  101.5 4.7 %copy-start.3 = (bf16[1024,1024]{1,0:T(8,128)(2,1)S(1)}, bf16[1024,1024]{1,0:T(8,128)(2,1)}, u32[]{:S(2)}) copy-start(bf16[1024,1024]{1,0:T(8,128)(2,1)} %param.7) | copy-start | bytes 6291460
Sparse Core Ops, SparseCore 0:
  55.1 36.3 all-gather.1
where the time goes:
time: 119 us; the launch traced here: 118 us
  waiting for transfers between devices  42.8 us (36%)
  blocking collectives  18.8 us (16%)
  between operations  16.3 us (14%)
  starting transfers between devices  11.5 us (10%)
  other arithmetic  11.4 us (10%)
  matrix products  8.89 us (7%)
  local copies, waits for them, and re-layouts  8.73 us (7%)
    all_to_all x1, waiting for transfers between devices, per_device(): lax.all_to_all(outgoing, 'table', split_axis=0, concat_axis=0, tiled=True)  24.9 us
    unnamed x1, blocking collectives  18.8 us
    all_gather x1, waiting for transfers between devices, per_device(): lax.all_gather(packed, 'dp', axis=0, tiled=True)  15 us
    all_to_all x1, starting transfers between devices, per_device(): lax.all_to_all(labels, 'table', split_axis=0, concat_axis=0, tiled=True)  7.58 us
    dot_general x1, matrix products, per_device(): jnp.einsum('bk,kxd->bxd', placing, all_packed, precision=lax.Precision.HI...  6.56 us
    select_n x1, other arithmetic, adam_rows(): new_values = jnp.where(touched, moved.astype(jnp.bfloat16), values)  5.21 us
    select_n x1, other arithmetic, adam_rows(): new_second = jnp.where(touched, second_next, second_moment)  4.72 us
    all_to_all x1, starting transfers between devices, per_device(): lax.all_to_all(outgoing, 'table', split_axis=0, concat_axis=0, tiled=True)  3.86 us
  transfers between devices with their start and end apart: 3, of which 3 were waited for; matrix products, arithmetic and copies ran while one was open for 5% of the time, Pallas kernels for 0%

commit v1 on v0

--- a/solution.py
+++ b/solution.py
@@ -61,8 +61,17 @@
     block_index = jnp.arange(blk_here, dtype=jnp.float32)
     packed_ids = jnp.sum(packing * (block_index[None, :] + 1.0), axis=1) - 1.0
     packed_hits = jnp.sum(packing * block_hits[None, :], axis=1)
+
+    def group_stocks_for(field_in, group_axis="dp"):
+        return jnp.concatenate(
+            lax.all_to_all(
+                jnp.stack([field_in] * lax.axis_size(group_axis), axis=0), group_axis, 0, 0
+            ),
+            axis=0,
+        )
+
     all_packed, all_ids, all_hits = (
-        lax.all_gather(packed, "dp", axis=0, tiled=True),
+        group_stocks_for(packed),
         lax.all_gather(packed_ids, "dp", axis=0, tiled=True),
         lax.all_gather(packed_hits, "dp", axis=0, tiled=True),
     )

time: 119 us -> 146 us (1.23)
  blocking collectives: 18.8 us -> 50.6 us
  local copies, waits for them, and re-layouts: 8.73 us -> 24.1 us
  waiting for transfers between devices: 42.8 us -> 27.9 us
  between operations: 16.3 us -> 2.87 us
  starting transfers between devices: 11.5 us -> 21.9 us
  matrix products: 8.89 us -> 6.59 us
    unnamed x1, blocking collectives: 18.8 us -> 50.6 us
    all_gather x1 -> x0, waiting for transfers between devices: 15 us -> none  [per_device(): lax.all_gather(packed, 'dp', axis=0, tiled=True)]
    all_to_all x0 -> x1, starting transfers between devices: none -> 10.6 us  [group_stocks_for(): lax.all_to_all(jnp.stack([field_in] * lax.axis_size(group_axis), axis=0),...]
    all_to_all x0 -> x1, local copies, waits for them, and re-layouts: none -> 6.82 us  [group_stocks_for(): lax.all_to_all(jnp.stack([field_in] * lax.axis_size(group_axis), axis=0),...]
    reshape x0 -> x1, local copies, waits for them, and re-layouts: none -> 6.04 us  [group_stocks_for(): jnp.concatenate(lax.all_to_all(jnp.stack([field_in] * lax.axis_size(group...]
    another operation x0 -> x1, local copies, waits for them, and re-layouts: none -> 3.45 us  [group_stocks_for(): jnp.stack([field_in] * lax.axis_size(group_axis), axis=0)]
    dot_general x1, matrix products: 6.56 us -> 4.26 us  [per_device(): jnp.einsum('bk,kxd->bxd', placing, all_packed, precision=lax.Precision.HI...]
  transfers between devices with their start and end apart: 3 -> 3, of which waited for: 3 -> 2; matrix products, arithmetic and copies ran while one was open for 5% -> 4% of each run, Pallas kernels for 0% -> 0%
where the time goes in v1:
time: 146 us; the launch traced here: 145 us
  blocking collectives  50.6 us (35%)
  waiting for transfers between devices  27.9 us (19%)
  local copies, waits for them, and re-layouts  24.1 us (17%)
  starting transfers between devices  21.9 us (15%)
  other arithmetic  11.4 us (8%)
  matrix products  6.59 us (5%)
  between operations  2.87 us (2%)
    unnamed x1, blocking collectives  50.6 us
    all_to_all x1, waiting for transfers between devices, per_device(): lax.all_to_all(outgoing, 'table', split_axis=0, concat_axis=0, tiled=True)  25 us
    all_to_all x1, starting transfers between devices, group_stocks_for(): lax.all_to_all(jnp.stack([field_in] * lax.axis_size(group_axis), axis=0),...  10.6 us
    all_to_all x1, starting transfers between devices, per_device(): lax.all_to_all(labels, 'table', split_axis=0, concat_axis=0, tiled=True)  7.58 us
    all_to_all x1, local copies, waits for them, and re-layouts, group_stocks_for(): lax.all_to_all(jnp.stack([field_in] * lax.axis_size(group_axis), axis=0),...  6.82 us
    reshape x1, local copies, waits for them, and re-layouts, group_stocks_for(): jnp.concatenate(lax.all_to_all(jnp.stack([field_in] * lax.axis_size(group...  6.04 us
    select_n x1, other arithmetic, adam_rows(): new_values = jnp.where(touched, moved.astype(jnp.bfloat16), values)  5.21 us
    select_n x1, other arithmetic, adam_rows(): new_second = jnp.where(touched, second_next, second_moment)  4.72 us
  transfers between devices with their start and end apart: 3, of which 2 were waited for; matrix products, arithmetic and copies ran while one was open for 4% of the time, Pallas kernels for 0%

profile of v1, /device:TPU:1, one launch (start us, length us, event | category | flops | bytes accessed | tf_op | source)
XLA Modules:
  0.0 145.3 jit_solution(3138446018042766129)
XLA Ops:
  0.6 0.0 copy-start
  1.4 0.7 fusion.23
  2.1 0.1 select_reduce_fusion.1
  2.2 0.7 copy.21
  2.8 7.6 %all-to-all-start = ((s32[16,1,2]{2,1,0:T(1,128)}), s32[16,1,2]{2,1,0:T(1,128)S(1)}, u32[]{:S(2)}, u32[]{:S(2)}) async-start(s32[16,1,2]{2,1,0:T(1,128)} %copy.21), calls=%async_computation | async-start | bytes 16384 | tf_op jit(solution)/shard_map/all_to_all | solution.py:46
  10.4 0.0 copy-done
  10.4 0.9 convolution_convert_fusion
  11.4 2.5 %copy.25 = bf16[16,64,1024]{2,1,0:T(8,128)(2,1)} copy(bf16[16,64,1024]{2,0,1:T(8,128)(2,1)S(1)} %convolution_convert_fusion) | data formatting | bytes 4194304 | tf_op jit(solution)/shard_map/convert_element_type | solution.py:39
  13.8 2.9 %all-to-all-done = s32[16,1,2]{2,1,0:T(1,128)S(1)} async-done(((s32[16,1,2]{2,1,0:T(1,128)}), s32[16,1,2]{2,1,0:T(1,128)S(1)}, u32[]{:S(2)}, u32[]{:S(2)}) %all-to-all-start) | async-done | bytes 160 | tf_op jit(solution)/shard_map/all_to_all | solution.py:46
  16.8 3.7 %all-to-all-start.1 = ((bf16[16,64,1024]{2,1,0:T(8,128)(2,1)}), bf16[16,64,1024]{2,1,0:T(8,128)(2,1)S(1)}, u32[]{:S(2)}, u32[]{:S(2)}) async-start(bf16[16,64,1024]{2,1,0:T(8,128)(2,1)} %copy.25), calls=%async_computation.1 | async-start | bytes 4194304 | tf_op jit(solution)/shard_map/all_to_all | solution.py:45
  20.5 0.1 copy.22
  20.6 0.1 convert_reduce_fusion
  20.7 0.1 copy.23
  20.9 0.1 add_reduce_fusion
  21.0 0.1 fusion.7
  21.1 25.0 %all-to-all-done.1 = bf16[16,64,1024]{2,1,0:T(8,128)(2,1)S(1)} async-done(((bf16[16,64,1024]{2,1,0:T(8,128)(2,1)}), bf16[16,64,1024]{2,1,0:T(8,128)(2,1)S(1)}, u32[]{:S(2)}, u32[]{:S(2)}) %all-to-all-start.1) | async-done | bytes 2097184 | tf_op jit(solution)/shard_map/all_to_all | solution.py:45
  46.1 1.3 fusion.5
  47.3 3.4 %stack.11 = f32[8,2,64,1024]{3,1,2,0:T(2,128)} broadcast(f32[2,64,1024]{2,0,1:T(2,128)S(1)} %fusion.5), dimensions={1,2,3} | broadcast | bytes 4718592 | tf_op jit(solution)/shard_map/stack | solution.py:68
  50.8 0.0 copy-start.4
  50.8 10.6 %all-to-all-start.2 = ((f32[8,2,64,1024]{3,1,2,0:T(2,128)}), f32[8,2,64,1024]{3,1,2,0:T(2,128)}, u32[]{:S(2)}, u32[]{:S(2)}) async-start(f32[8,2,64,1024]{3,1,2,0:T(2,128)} %stack.11), calls=%async_computation.2 | async-start | bytes 8388608 | tf_op jit(solution)/shard_map/all_to_all | solution.py:67
  62.1 0.0 copy-done.4
  62.1 0.6 dynamic-slice
  63.4 0.1 select_reduce_fusion.2
  63.5 0.2 dynamic-update-slice.1
  63.8 0.1 add_dynamic-update-slice_fusion
  63.9 50.6 %all-reduce.2 = (f32[16]{0:T(128)S(1)}, f32[16]{0:T(128)S(1)}) all-reduce(f32[16]{0:T(128)S(1)} %add_dynamic-update-slice_fusion, f32[16]{0:T(128)S(1)} %dynamic-update-slice.1), channel_id=1, replica_groups=mesh['dp'=8,'table'=16] {'dp'}, use_global_device_ids=true, to_apply=%add | all-reduce | flops 32 | bytes 256
  114.4 0.1 select_reduce_fusion
  114.6 0.1 broadcast_in_dim.13
  114.7 0.1 gt.31
  114.7 0.0 all-to-all-done.2
  114.7 6.8 %copy.27 = f32[8,2,64,1024]{3,1,0,2:T(2,128)} copy(f32[8,2,64,1024]{3,1,2,0:T(2,128)} %all-to-all-done.2) | data formatting | bytes 8388608 | tf_op jit(solution)/shard_map/all_to_all | solution.py:67
  121.6 6.0 %reshape.95 = f32[16,64,1024]{2,0,1:T(8,128)} reshape(f32[8,2,64,1024]{3,1,0,2:T(2,128)} %copy.27) | data formatting | bytes 8388608 | tf_op jit(solution)/shard_map/reshape | solution.py:66
  127.6 4.3 %fusion.12 = f32[16,64,1024]{2,0,1:T(8,128)S(1)} fusion(f32[16,64,1024]{2,0,1:T(8,128)} %reshape.95, f32[16]{0:T(128)S(1)} %get-tuple-element.7), kind=kOutput, calls=%fused_computation.21 | convolution fusion | flops 201326848 | bytes 8388672 | tf_op jit(solution)/shard_map/bk,kxd->bxd/dot_general | solution.py:79
  131.9 0.0 copy-start.1
  131.9 0.0 copy-start.2
  131.9 2.4 %copy.28 = f32[16,64,1024]{2,1,0:T(8,128)S(1)} copy(f32[16,64,1024]{2,0,1:T(8,128)S(1)} %fusion.12) | data formatting | bytes 8388608 | tf_op jit(solution)/shard_map/bk,kxd->bxd/dot_general | solution.py:79
  134.3 0.0 copy-done.1
  134.3 1.0 copy-done.2
  135.3 0.0 copy-start.3
  135.3 4.7 %fusion.3 = (f32[1024,1024]{1,0:T(8,128)}, f32[1024,1024]{1,0:T(8,128)}) fusion(f32[1024,1024]{1,0:T(8,128)S(1)} %copy-done.1, f32[16,64,1024]{2,1,0:T(8,128)S(1)} %copy.28, pred[1024]{0:T(1024)(128)(4,1)S(1)} %gt.31, f32[1024,1024]{1,0:T(8,128)S(1)} %copy-done.2), kind=kLoop, calls=%fused_computation.6 | loop fusion | flops 9437184 | bytes 20972544 | tf_op jit(solution)/shard_map/jit(_where)/select_n | solution.py:23
  140.1 0.0 copy-done.3
  140.1 5.2 %fusion.4 = bf16[1024,1024]{1,0:T(8,128)(2,1)} fusion(bf16[1024,1024]{1,0:T(8,128)(2,1)S(1)} %copy-done.3, f32[1024,1024]{1,0:T(8,128)S(1)} %copy-done.1, f32[16,64,1024]{2,1,0:T(8,128)S(1)} %copy.28, f32[1024,1024]{1,0:T(8,128)S(1)} %copy-done.2, f32[]{:T(128)} %bitcast.16, f32[]{:T(128)} %bitcast.15, pred[1024]{0:T(1024)(128)(4,1)S(1)} %gt.31), kind=kLoop, calls=%fused_computation.7 | loop fusion | flops 16777216 | bytes 16778248 | tf_op jit(solution)/shard_map/jit(_where)/select_n | solution.py:21
  (10 shorter events, 0.1 us)
Async XLA Ops:
  0.6 9.8 %copy-start = (bf16[8,64,1024]{2,1,0:T(8,128)(2,1)S(1)}, bf16[8,64,1024]{2,1,0:T(8,128)(2,1)}, u32[]{:S(2)}) copy-start(bf16[8,64,1024]{2,1,0:T(8,128)(2,1)} %param.10) | copy-start | bytes 3145732
  2.8 13.9 %all-to-all-start = ((s32[16,1,2]{2,1,0:T(1,128)}), s32[16,1,2]{2,1,0:T(1,128)S(1)}, u32[]{:S(2)}, u32[]{:S(2)}) async-start(s32[16,1,2]{2,1,0:T(1,128)} %copy.21), calls=%async_computation | async-start | bytes 16384 | tf_op jit(solution)/shard_map/all_to_all | solution.py:46
  16.8 29.3 %all-to-all-start.1 = ((bf16[16,64,1024]{2,1,0:T(8,128)(2,1)}), bf16[16,64,1024]{2,1,0:T(8,128)(2,1)S(1)}, u32[]{:S(2)}, u32[]{:S(2)}) async-start(bf16[16,64,1024]{2,1,0:T(8,128)(2,1)} %copy.25), calls=%async_computation.1 | async-start | bytes 4194304 | tf_op jit(solution)/shard_map/all_to_all | solution.py:45
  50.8 11.3 %copy-start.4 = (u32[128]{0:T(128)S(1)}, u32[128]{0:T(128)}, u32[]{:S(2)}) copy-start(u32[128]{0:T(128)} %constant.75) | copy-start | bytes 1540
  50.8 63.9 %all-to-all-start.2 = ((f32[8,2,64,1024]{3,1,2,0:T(2,128)}), f32[8,2,64,1024]{3,1,2,0:T(2,128)}, u32[]{:S(2)}, u32[]{:S(2)}) async-start(f32[8,2,64,1024]{3,1,2,0:T(2,128)} %stack.11), calls=%async_computation.2 | async-start | bytes 8388608 | tf_op jit(solution)/shard_map/all_to_all | solution.py:67
  131.9 2.5 %copy-start.1 = (f32[1024,1024]{1,0:T(8,128)S(1)}, f32[1024,1024]{1,0:T(8,128)}, u32[]{:S(2)}) copy-start(f32[1024,1024]{1,0:T(8,128)} %param.9) | copy-start | bytes 12582916
  131.9 3.5 %copy-start.2 = (f32[1024,1024]{1,0:T(8,128)S(1)}, f32[1024,1024]{1,0:T(8,128)}, u32[]{:S(2)}) copy-start(f32[1024,1024]{1,0:T(8,128)} %param.8) | copy-start | bytes 12582916
  135.3 4.7 %copy-start.3 = (bf16[1024,1024]{1,0:T(8,128)(2,1)S(1)}, bf16[1024,1024]{1,0:T(8,128)(2,1)}, u32[]{:S(2)}) copy-start(bf16[1024,1024]{1,0:T(8,128)(2,1)} %param.7) | copy-start | bytes 6291460
